TPU v7x, 512 devices: a whole 4x4x16 slice. The times are simulated.
512 devices in a mesh: rows: 64 (over y, z), cols: 8 (over x, core).
Axes of the slice: x: 4, y: 4, z: 16, core: 2. Of those that a mesh axis runs over, the one named last changes fastest.
Arguments:
- node_features: bfloat16 [65536, 512], P('rows', 'cols'), may hold values from -6 to 6
- weight: bfloat16 [512, 512], replicated, may hold values from -0.25 to 0.25
- tile_values: bfloat16 [4096, 128, 128], P('rows'), may hold values from -0.1875 to 0.1875
- tile_row: int32 [4096], P('rows'), may hold values from 0 to 7
- source_owner: int32 [4096, 1], P('rows'), may hold values from 0 to 63; in each aligned block of 64 rows (0 to 63, 64 to 127, ...) at most 2 rows name the same one
- source_block: int32 [4096], P('rows'), may hold values from 0 to 7
- labels: int32 [65536], P('rows'), may hold values from 0 to 511
Outputs:
- activations: bfloat16 [65536, 512], P('rows', 'cols')
- weight_grad: float32 [512, 512], P(None, 'cols')
- feature_grad: bfloat16 [65536, 512], P('rows', 'cols')
Inputs may be any that keep to these rules, and one draw needn't show every extreme that they name: `source_owner`: of the 64 tiles of one index of rows, at most 2 name the same owner.
All inputs are finite; a program needn't handle non-finite values.
Results may differ from a plain program's by a relative error of at most 0.0095.
Values may be sent and summed in bfloat16 or wider, within the bound.
A program may use at most 64 MiB of HBM per device.

v0:
```python
import math
import jax
import jax.numpy as jnp
from jax import lax
from jax.sharding import PartitionSpec as P


def slot_ranks(owners):
    positions = jnp.arange(owners.shape[0], dtype=jnp.int32)
    earlier = (owners[:, None] == owners[None, :]) & (positions[None, :] < positions[:, None])
    return jnp.sum(earlier.astype(jnp.int32), axis=1)


def rows_exchange(x):
    return lax.all_to_all(x, "rows", split_axis=0, concat_axis=0, tiled=True)


def row_all_reduce(partial):
    row_devices = lax.axis_size("rows")
    k, c = partial.shape
    pieces = partial.reshape(row_devices, k // row_devices, c)
    reduced = jnp.sum(rows_exchange(pieces), axis=0)
    return lax.all_gather(reduced, "rows", axis=0, tiled=True)


def per_device(node_features, weight, tile_values, tile_row, source_owner, source_block, labels):
    local_rows, col_width = node_features.shape
    block_size = tile_values.shape[1]
    local_blocks = local_rows // block_size
    row_devices = lax.axis_size("rows")
    col_devices = lax.axis_size("cols")
    tiles = tile_values.shape[0]
    capacity = 2 * tiles // row_devices
    half = col_width // 2
    owners = source_owner[:, 0]
    slot_rank = slot_ranks(owners)
    local_ids = jnp.arange(local_blocks, dtype=jnp.int32)
    row_onehot = (tile_row[:, None] == local_ids[None, :]).astype(jnp.float32)
    tile_ids = jnp.arange(tiles, dtype=jnp.int32)
    in_slot = (owners[:, None, None] == jnp.arange(row_devices, dtype=jnp.int32)[None, :, None]) & (
        slot_rank[:, None, None] == jnp.arange(capacity, dtype=jnp.int32)[None, None, :]
    )
    request = jnp.sum(jnp.where(in_slot, source_block[:, None, None], 0), axis=0)
    slot_tile = jnp.sum(jnp.where(in_slot, tile_ids[:, None, None] - tiles, 0), axis=0) + tiles
    wanted = rows_exchange(request)
    own_blocks = node_features.reshape(local_blocks, block_size, col_width)
    outgoing = own_blocks[wanted]
    col_index = lax.axis_index("cols")
    w_columns = lax.dynamic_slice_in_dim(weight, col_index * col_width, col_width, 1)
    w_rows = lax.dynamic_slice_in_dim(weight, col_index * col_width, col_width, 0)
    w_split = w_columns.reshape(col_devices, col_width, col_width)

    def aggregate(part):
        source_rows = part[owners, slot_rank]
        products = jnp.einsum(
            "tij,tjf->tif", tile_values, source_rows, preferred_element_type=jnp.float32
        )
        summed = jnp.einsum("tb,tif->bif", row_onehot, products, precision=lax.Precision.HIGHEST)
        return summed.reshape(local_rows, part.shape[-1]).astype(jnp.bfloat16)

    first = aggregate(rows_exchange(outgoing[..., :half]))
    second_out, first = lax.optimization_barrier((outgoing[..., half:], first))
    first_all = lax.all_gather(first, "cols", axis=0, tiled=False)
    second = aggregate(rows_exchange(second_out))
    second_all = lax.all_gather(second, "cols", axis=0, tiled=False)
    hidden = jnp.einsum(
        "jnf,jfc->nc", first_all, w_split[:, :half], preferred_element_type=jnp.float32
    ) + jnp.einsum("jnf,jfc->nc", second_all, w_split[:, half:], preferred_element_type=jnp.float32)
    sigmoid = jax.nn.sigmoid(hidden)
    activated = hidden * sigmoid
    slopes = sigmoid * (1.0 + hidden * (1.0 - sigmoid))
    feature_ids = col_index * col_width + jnp.arange(col_width, dtype=jnp.int32)
    target = (labels[:, None] == feature_ids[None, :]).astype(jnp.float32)
    out_grad = ((activated - target) * slopes).astype(jnp.bfloat16)
    grad_all = lax.all_gather(out_grad, "cols", axis=1, tiled=True)
    weight_terms = jnp.concatenate(
        [
            jnp.einsum("jnf,nc->jfc", first_all, out_grad, preferred_element_type=jnp.float32),
            jnp.einsum("jnf,nc->jfc", second_all, out_grad, preferred_element_type=jnp.float32),
        ],
        axis=1,
    ).reshape(col_devices * col_width, col_width)
    node_total = local_rows * row_devices
    weight_grad = row_all_reduce(weight_terms) / math.sqrt(node_total)
    agg_grad = jnp.einsum("nc,kc->nk", grad_all, w_rows, preferred_element_type=jnp.float32).astype(
        jnp.bfloat16
    )
    grad_rows = agg_grad.reshape(local_blocks, block_size, col_width)[tile_row]
    sent_terms = jnp.einsum(
        "tji,tjf->tif", tile_values, grad_rows, preferred_element_type=jnp.float32
    ).astype(jnp.bfloat16)
    padded_terms = jnp.concatenate([sent_terms, jnp.zeros_like(sent_terms[:1])], axis=0)
    received = rows_exchange(padded_terms[slot_tile])
    placing = (wanted[:, :, None] == local_ids[None, None, :]).astype(jnp.float32)
    feature_grad = jnp.einsum(
        "scb,scif->bif", placing, received.astype(jnp.float32), precision=lax.Precision.HIGHEST
    ).reshape(local_rows, col_width)
    return (activated.astype(jnp.bfloat16), weight_grad, feature_grad.astype(jnp.bfloat16))


def solution(mesh):
    return jax.shard_map(
        per_device,
        mesh=mesh,
        in_specs=(
            P("rows", "cols"),
            P(),
            P("rows", None, None),
            P("rows"),
            P("rows", None),
            P("rows"),
            P("rows"),
        ),
        out_specs=(P("rows", "cols"), P(None, "cols"), P("rows", "cols")),
        check_vma=False,
    )
```

profile of v0, /device:TPU:8, one launch (start us, length us, event | category | flops | bytes accessed | tf_op | source)
XLA Modules:
  0.0 418.3 jit_solution(6826741657737070376)
XLA Ops:
  7.2 1.0 convert_reduce_fusion
  10.4 18.7 %all-to-all-start = ((s32[64,1,2]{2,1,0:T(1,128)}), s32[64,1,2]{2,1,0:T(1,128)S(1)}, u32[]{:S(2)}, u32[]{:S(2)}) async-start(s32[64,1,2]{2,1,0:T(1,128)} %copy.57), calls=%async_computation | async-start | bytes 65536 | tf_op jit(solution)/shard_map/all_to_all | solution.py:15
  29.2 0.9 copy_bitcast_fusion.2
  30.1 12.5 %all-to-all-done = s32[64,1,2]{2,1,0:T(1,128)S(1)} async-done(((s32[64,1,2]{2,1,0:T(1,128)}), s32[64,1,2]{2,1,0:T(1,128)S(1)}, u32[]{:S(2)}, u32[]{:S(2)}) %all-to-all-start) | async-done | bytes 544 | tf_op jit(solution)/shard_map/all_to_all | solution.py:15
  43.0 2.2 gather_fusion
  45.1 3.3 fusion.40
  48.4 6.5 %all-to-all-start.1 = ((bf16[64,2,128,32]{2,3,1,0:T(8,128)(2,1)}), bf16[64,2,128,32]{2,3,1,0:T(8,128)(2,1)}, u32[]{:S(2)}, u32[]{:S(2)}) async-start(bf16[64,2,128,32]{2,3,1,0:T(8,128)(2,1)} %get-tuple-element.15), calls=%async_computation.1 | async-start | bytes 2097152 | tf_op jit(solution)/shard_map/all_to_all | solution.py:15
  54.9 52.2 %all-to-all-done.1 = bf16[64,2,128,32]{2,3,1,0:T(8,128)(2,1)} async-done(((bf16[64,2,128,32]{2,3,1,0:T(8,128)(2,1)}), bf16[64,2,128,32]{2,3,1,0:T(8,128)(2,1)}, u32[]{:S(2)}, u32[]{:S(2)}) %all-to-all-start.1) | async-done | bytes 1048608 | tf_op jit(solution)/shard_map/all_to_all | solution.py:15
  107.1 2.0 gather_fusion.1
  109.0 1.2 convolution_bitcast_fusion.1
  110.2 1.1 convolution_convert_fusion.3
  111.3 7.4 %all-to-all-start.2 = ((bf16[64,2,128,32]{2,3,1,0:T(8,128)(2,1)}), bf16[64,2,128,32]{2,3,1,0:T(8,128)(2,1)}, u32[]{:S(2)}, u32[]{:S(2)}) async-start(bf16[64,2,128,32]{2,3,1,0:T(8,128)(2,1)} %get-tuple-element.6), calls=%async_computation.2 | async-start | bytes 2097152 | tf_op jit(solution)/shard_map/all_to_all | solution.py:15
  118.8 1.0 constant_dynamic-slice_fusion
  119.9 13.5 %all-gather = bf16[8192,32]{0,1:T(8,128)(2,1)S(1)} all-gather(bf16[1024,32]{0,1:T(8,128)(2,1)S(1)} %bitcast.101), channel_id=2, replica_groups=mesh['rows'=64,'cols'=8] {'cols'}, dimensions={0}, use_global_device_ids=true | all-gather | bytes 589824 | tf_op jit(solution)/shard_map/all_gather | solution.py:63
  133.6 38.6 %all-to-all-done.2 = bf16[64,2,128,32]{2,3,1,0:T(8,128)(2,1)} async-done(((bf16[64,2,128,32]{2,3,1,0:T(8,128)(2,1)}), bf16[64,2,128,32]{2,3,1,0:T(8,128)(2,1)}, u32[]{:S(2)}, u32[]{:S(2)}) %all-to-all-start.2) | async-done | bytes 1048608 | tf_op jit(solution)/shard_map/all_to_all | solution.py:15
  172.2 2.0 gather_fusion.2
  174.1 1.2 convolution_bitcast_fusion
  175.3 1.1 convolution_convert_fusion.2
  176.4 13.5 %all_gather.18 = bf16[8,1024,32]{1,2,0:T(8,128)(2,1)S(1)} all-gather(bf16[1,1024,32]{1,2,0:T(8,128)(2,1)S(1)} %convert_element_type.53), channel_id=1, replica_groups=mesh['rows'=64,'cols'=8] {'cols'}, dimensions={0}, use_global_device_ids=true | all-gather | bytes 589824 | tf_op jit(solution)/shard_map/all_gather | solution.py:65
  190.2 1.0 multiply_convert_fusion
  191.5 1.2 fusion.15
  192.8 1.2 fusion.17
  194.1 0.8 reshape.206
  194.9 6.9 %all-to-all-start.3 = ((f32[64,1,512]{2,1,0:T(1,128)}), f32[64,1,512]{2,1,0:T(1,128)S(1)}, u32[]{:S(2)}, u32[]{:S(2)}) async-start(f32[64,1,512]{2,1,0:T(1,128)} %reshape.206), calls=%async_computation.3 | async-start | bytes 262144 | tf_op jit(solution)/shard_map/all_to_all | solution.py:15
  201.8 12.5 %all-gather.3.cloned.1.call-done = bf16[1024,512]{0,1:T(8,128)(2,1)} async-done(((bf16[1024,64]{0,1:T(8,128)(2,1)}), bf16[1024,512]{0,1:T(8,128)(2,1)}) %all-gather.3.cloned.1.call-update) | async-done | bytes 1048592 | tf_op jit(solution)/shard_map/all_gather | solution.py:75
  214.3 1.6 fusion.10
  217.4 2.1 gather_fusion.4
  219.5 5.1 %copy.71 = bf16[64,2,128,64]{2,1,3,0:T(2,128)(2,1)} copy(bf16[64,2,128,64]{2,3,1,0:T(8,128)(2,1)} %bitcast.93) | data formatting | bytes 4194304 | tf_op jit(solution)/shard_map/gather | solution.py:93
  224.6 15.9 %all-to-all-start.4 = ((bf16[64,2,128,64]{2,1,3,0:T(2,128)(2,1)}), bf16[64,2,128,64]{2,1,3,0:T(2,128)(2,1)}, u32[]{:S(2)}, u32[]{:S(2)}) async-start(bf16[64,2,128,64]{2,1,3,0:T(2,128)(2,1)} %copy.71), calls=%async_computation.4 | async-start | bytes 4194304 | tf_op jit(solution)/shard_map/all_to_all | solution.py:15
  241.1 0.9 reduce
  242.2 163.9 %all_gather.19 = f32[512,64]{1,0:T(8,128)S(1)} all-gather(f32[8,64]{1,0:T(8,128)S(1)} %reduce_sum.41), channel_id=1, replica_groups=mesh['rows'=64,'cols'=8] {'rows'}, dimensions={0}, use_global_device_ids=true | all-gather | bytes 133120 | tf_op jit(solution)/shard_map/all_gather | solution.py:23
  406.9 3.9 fusion.7
  (48 shorter events, 7.3 us)
Async XLA Ops:
  7.2 101.9 %copy-start = (bf16[64,128,128]{2,1,0:T(8,128)(2,1)S(1)}, bf16[64,128,128]{2,1,0:T(8,128)(2,1)}, u32[]{:S(2)}) copy-start(bf16[64,128,128]{2,1,0:T(8,128)(2,1)} %param.9) | copy-start | bytes 6291460
  10.4 32.2 %all-to-all-start = ((s32[64,1,2]{2,1,0:T(1,128)}), s32[64,1,2]{2,1,0:T(1,128)S(1)}, u32[]{:S(2)}, u32[]{:S(2)}) async-start(s32[64,1,2]{2,1,0:T(1,128)} %copy.57), calls=%async_computation | async-start | bytes 65536 | tf_op jit(solution)/shard_map/all_to_all | solution.py:15
  48.4 6.5 %copy-start.2 = (s32[64,1]{0,1:T(1,128)S(1)}, s32[64,1]{0,1:T(1,128)}, u32[]{:S(2)}) copy-start(s32[64,1]{0,1:T(1,128)} %param.11) | copy-start | bytes 772
  48.4 58.7 %all-to-all-start.1 = ((bf16[64,2,128,32]{2,3,1,0:T(8,128)(2,1)}), bf16[64,2,128,32]{2,3,1,0:T(8,128)(2,1)}, u32[]{:S(2)}, u32[]{:S(2)}) async-start(bf16[64,2,128,32]{2,3,1,0:T(8,128)(2,1)} %get-tuple-element.15), calls=%async_computation.1 | async-start | bytes 2097152 | tf_op jit(solution)/shard_map/all_to_all | solution.py:15
  109.0 1.2 copy-start.1
  111.3 60.9 %all-to-all-start.2 = ((bf16[64,2,128,32]{2,3,1,0:T(8,128)(2,1)}), bf16[64,2,128,32]{2,3,1,0:T(8,128)(2,1)}, u32[]{:S(2)}, u32[]{:S(2)}) async-start(bf16[64,2,128,32]{2,3,1,0:T(8,128)(2,1)} %get-tuple-element.6), calls=%async_computation.2 | async-start | bytes 2097152 | tf_op jit(solution)/shard_map/all_to_all | solution.py:15
  118.8 95.5 %all-gather.3.cloned.1.call-start = ((), (), s32[]{:S(2)}) async-start(), calls=%async_computation.5 | async-start | bytes 1179648 | tf_op jit(solution)/shard_map/all_gather | solution.py:75
  175.3 14.8 %copy-start.3 = (s32[1024]{0:T(1024)S(1)}, s32[1024]{0:T(1024)}, u32[]{:S(2)}) copy-start(s32[1024]{0:T(1024)} %param.13) | copy-start | bytes 12292
  194.9 29.7 %all-to-all-start.3 = ((f32[64,1,512]{2,1,0:T(1,128)}), f32[64,1,512]{2,1,0:T(1,128)S(1)}, u32[]{:S(2)}, u32[]{:S(2)}) async-start(f32[64,1,512]{2,1,0:T(1,128)} %reshape.206), calls=%async_computation.3 | async-start | bytes 262144 | tf_op jit(solution)/shard_map/all_to_all | solution.py:15
  224.6 182.2 %all-to-all-start.4 = ((bf16[64,2,128,64]{2,1,3,0:T(2,128)(2,1)}), bf16[64,2,128,64]{2,1,3,0:T(2,128)(2,1)}, u32[]{:S(2)}, u32[]{:S(2)}) async-start(bf16[64,2,128,64]{2,1,3,0:T(2,128)(2,1)} %copy.71), calls=%async_computation.4 | async-start | bytes 4194304 | tf_op jit(solution)/shard_map/all_to_all | solution.py:15
Sparse Core Ops, SparseCore 0:
  191.3 22.9 all-gather.2
where the time goes:
time: 419 us; the launch traced here: 418 us
  blocking collectives  191 us (46%)
  waiting for transfers between devices  116 us (28%)
  starting transfers between devices  55.5 us (13%)
  local copies, waits for them, and re-layouts  24 us (6%)
  between operations  14.4 us (3%)
  matrix products  14.3 us (3%)
    all_gather x1, blocking collectives, row_all_reduce(): return lax.all_gather(reduced, 'rows', axis=0, tiled=True)  164 us
    all_to_all x5, waiting for transfers between devices, rows_exchange(): return lax.all_to_all(x, 'rows', split_axis=0, concat_axis=0, tiled=True)  103 us
    all_to_all x5, starting transfers between devices, rows_exchange(): return lax.all_to_all(x, 'rows', split_axis=0, concat_axis=0, tiled=True)  55.4 us
    all_gather x1, blocking collectives, per_device(): first_all = lax.all_gather(first, 'cols', axis=0, tiled=False)  13.5 us
    all_gather x1, blocking collectives, per_device(): second_all = lax.all_gather(second, 'cols', axis=0, tiled=False)  13.5 us
    all_gather x1, waiting for transfers between devices, per_device(): grad_all = lax.all_gather(out_grad, 'cols', axis=1, tiled=True)  12.5 us
  transfers between devices with their start and end apart: 6, of which 4 were waited for; matrix products, arithmetic and copies ran while one was open for 4% of the time, Pallas kernels for 0%

commit v1 on v0

--- a/solution.py
+++ b/solution.py
@@ -20,7 +20,9 @@
     k, c = partial.shape
     pieces = partial.reshape(row_devices, k // row_devices, c)
     reduced = jnp.sum(rows_exchange(pieces), axis=0)
-    return lax.all_gather(reduced, "rows", axis=0, tiled=True)
+    return jnp.concatenate(
+        lax.all_to_all(jnp.stack([reduced] * lax.axis_size("rows")), "rows", 0, 0), axis=0
+    )
 
 
 def per_device(node_features, weight, tile_values, tile_row, source_owner, source_block, labels):

time: 419 us -> 362 us (0.86)
  blocking collectives: 191 us -> 26.9 us
  waiting for transfers between devices: 116 us -> 220 us
    all_gather x1 -> x0, blocking collectives: 164 us -> none  [row_all_reduce(): return lax.all_gather(reduced, 'rows', axis=0, tiled=True)]
    all_to_all x5, waiting for transfers between devices: 103 us -> 215 us  [rows_exchange(): return lax.all_to_all(x, 'rows', split_axis=0, concat_axis=0, tiled=True)]
    all_gather x1, waiting for transfers between devices: 12.5 us -> 0.02 us  [per_device(): grad_all = lax.all_gather(out_grad, 'cols', axis=1, tiled=True)]
    all_to_all x0 -> x1, starting transfers between devices: none -> 6.25 us  [row_all_reduce(): lax.all_to_all(jnp.stack([reduced] * lax.axis_size('rows')), 'rows', 0, 0)]
    all_to_all x5, starting transfers between devices: 55.4 us -> 49.8 us  [rows_exchange(): return lax.all_to_all(x, 'rows', split_axis=0, concat_axis=0, tiled=True)]
    all_to_all x0 -> x1, waiting for transfers between devices: none -> 5.04 us  [row_all_reduce(): lax.all_to_all(jnp.stack([reduced] * lax.axis_size('rows')), 'rows', 0, 0)]
  transfers between devices with their start and end apart: 6 -> 7, of which waited for: 4 -> 6; matrix products, arithmetic and copies ran while one was open for 4% -> 6% of each run, Pallas kernels for 0% -> 0%
where the time goes in v1:
time: 362 us; the launch traced here: 361 us
  waiting for transfers between devices  220 us (61%)
  starting transfers between devices  56.1 us (15%)
  blocking collectives  26.9 us (7%)
  local copies, waits for them, and re-layouts  25 us (7%)
  between operations  14.4 us (4%)
  matrix products  14.3 us (4%)
  other arithmetic  4.64 us (1%)
    all_to_all x5, waiting for transfers between devices, rows_exchange(): return lax.all_to_all(x, 'rows', split_axis=0, concat_axis=0, tiled=True)  215 us
    all_to_all x5, starting transfers between devices, rows_exchange(): return lax.all_to_all(x, 'rows', split_axis=0, concat_axis=0, tiled=True)  49.8 us
    all_gather x1, blocking collectives, per_device(): first_all = lax.all_gather(first, 'cols', axis=0, tiled=False)  13.5 us
    all_gather x1, blocking collectives, per_device(): second_all = lax.all_gather(second, 'cols', axis=0, tiled=False)  13.5 us
  transfers between devices with their start and end apart: 7, of which 6 were waited for; matrix products, arithmetic and copies ran while one was open for 6% of the time, Pallas kernels for 0%

profile of v1, /device:TPU:8, one launch (start us, length us, event | category | flops | bytes accessed | tf_op | source)
XLA Modules:
  0.0 361.1 jit_solution(18230123403996624552)
XLA Ops:
  7.2 1.0 convert_reduce_fusion
  10.4 18.7 %all-to-all-start = ((s32[64,1,2]{2,1,0:T(1,128)}), s32[64,1,2]{2,1,0:T(1,128)S(1)}, u32[]{:S(2)}, u32[]{:S(2)}) async-start(s32[64,1,2]{2,1,0:T(1,128)} %copy.60), calls=%async_computation | async-start | bytes 65536 | tf_op jit(solution)/shard_map/all_to_all | solution.py:15
  30.1 12.5 %all-to-all-done = s32[64,1,2]{2,1,0:T(1,128)S(1)} async-done(((s32[64,1,2]{2,1,0:T(1,128)}), s32[64,1,2]{2,1,0:T(1,128)S(1)}, u32[]{:S(2)}, u32[]{:S(2)}) %all-to-all-start) | async-done | bytes 544 | tf_op jit(solution)/shard_map/all_to_all | solution.py:15
  43.0 2.1 gather_fusion
  45.1 3.3 fusion.40
  48.4 6.5 %all-to-all-start.1 = ((bf16[64,2,128,32]{2,3,1,0:T(8,128)(2,1)}), bf16[64,2,128,32]{2,3,1,0:T(8,128)(2,1)}, u32[]{:S(2)}, u32[]{:S(2)}) async-start(bf16[64,2,128,32]{2,3,1,0:T(8,128)(2,1)} %get-tuple-element.24), calls=%async_computation.1 | async-start | bytes 2097152 | tf_op jit(solution)/shard_map/all_to_all | solution.py:15
  54.9 52.2 %all-to-all-done.1 = bf16[64,2,128,32]{2,3,1,0:T(8,128)(2,1)} async-done(((bf16[64,2,128,32]{2,3,1,0:T(8,128)(2,1)}), bf16[64,2,128,32]{2,3,1,0:T(8,128)(2,1)}, u32[]{:S(2)}, u32[]{:S(2)}) %all-to-all-start.1) | async-done | bytes 1048608 | tf_op jit(solution)/shard_map/all_to_all | solution.py:15
  107.1 2.0 gather_fusion.1
  109.0 1.2 convolution_bitcast_fusion.1
  110.2 1.1 convolution_convert_fusion.3
  111.3 7.4 %all-to-all-start.2 = ((bf16[64,2,128,32]{2,3,1,0:T(8,128)(2,1)}), bf16[64,2,128,32]{2,3,1,0:T(8,128)(2,1)}, u32[]{:S(2)}, u32[]{:S(2)}) async-start(bf16[64,2,128,32]{2,3,1,0:T(8,128)(2,1)} %get-tuple-element.6), calls=%async_computation.2 | async-start | bytes 2097152 | tf_op jit(solution)/shard_map/all_to_all | solution.py:15
  118.8 1.0 constant_dynamic-slice_fusion
  119.9 13.5 %all-gather = bf16[8192,32]{0,1:T(8,128)(2,1)S(1)} all-gather(bf16[1024,32]{0,1:T(8,128)(2,1)S(1)} %bitcast.103), channel_id=2, replica_groups=mesh['rows'=64,'cols'=8] {'cols'}, dimensions={0}, use_global_device_ids=true | all-gather | bytes 589824 | tf_op jit(solution)/shard_map/all_gather | solution.py:65
  133.6 38.6 %all-to-all-done.2 = bf16[64,2,128,32]{2,3,1,0:T(8,128)(2,1)} async-done(((bf16[64,2,128,32]{2,3,1,0:T(8,128)(2,1)}), bf16[64,2,128,32]{2,3,1,0:T(8,128)(2,1)}, u32[]{:S(2)}, u32[]{:S(2)}) %all-to-all-start.2) | async-done | bytes 1048608 | tf_op jit(solution)/shard_map/all_to_all | solution.py:15
  172.2 2.0 gather_fusion.2
  174.1 1.2 convolution_bitcast_fusion
  175.3 1.1 convolution_convert_fusion.2
  176.4 13.5 %all_gather.15 = bf16[8,1024,32]{1,2,0:T(8,128)(2,1)S(1)} all-gather(bf16[1,1024,32]{1,2,0:T(8,128)(2,1)S(1)} %convert_element_type.53), channel_id=1, replica_groups=mesh['rows'=64,'cols'=8] {'cols'}, dimensions={0}, use_global_device_ids=true | all-gather | bytes 589824 | tf_op jit(solution)/shard_map/all_gather | solution.py:67
  190.2 1.0 multiply_convert_fusion
  191.2 1.2 fusion.15
  192.5 1.2 fusion.17
  194.6 6.9 %all-to-all-start.3 = ((f32[64,1,512]{2,1,0:T(1,128)}), f32[64,1,512]{2,1,0:T(1,128)S(1)}, u32[]{:S(2)}, u32[]{:S(2)}) async-start(f32[64,1,512]{2,1,0:T(1,128)} %reshape.211), calls=%async_computation.3 | async-start | bytes 262144 | tf_op jit(solution)/shard_map/all_to_all | solution.py:15
  201.8 15.9 %all-to-all-done.3 = f32[64,1,512]{2,1,0:T(1,128)S(1)} async-done(((f32[64,1,512]{2,1,0:T(1,128)}), f32[64,1,512]{2,1,0:T(1,128)S(1)}, u32[]{:S(2)}, u32[]{:S(2)}) %all-to-all-start.3) | async-done | bytes 131104 | tf_op jit(solution)/shard_map/all_to_all | solution.py:15
  220.2 6.3 %all-to-all-start.4 = ((f32[64,1,512]{2,1,0:T(1,128)}), f32[64,1,512]{2,1,0:T(1,128)S(1)}, u32[]{:S(2)}, u32[]{:S(2)}) async-start(f32[64,1,512]{2,1,0:T(1,128)} %reshape.213), calls=%async_computation.4 | async-start | bytes 262144 | tf_op jit(solution)/shard_map/all_to_all | solution.py:24
  226.6 1.6 fusion.10
  229.7 2.1 gather_fusion.4
  231.8 5.1 %copy.74 = bf16[64,2,128,64]{2,1,3,0:T(2,128)(2,1)} copy(bf16[64,2,128,64]{2,3,1,0:T(8,128)(2,1)} %bitcast.95) | data formatting | bytes 4194304 | tf_op jit(solution)/shard_map/gather | solution.py:95
  236.9 5.0 %all-to-all-done.4 = f32[64,1,512]{2,1,0:T(1,128)S(1)} async-done(((f32[64,1,512]{2,1,0:T(1,128)}), f32[64,1,512]{2,1,0:T(1,128)S(1)}, u32[]{:S(2)}, u32[]{:S(2)}) %all-to-all-start.4) | async-done | bytes 131104 | tf_op jit(solution)/shard_map/all_to_all | solution.py:24
  241.9 10.3 %all-to-all-start.5 = ((bf16[64,2,128,64]{2,1,3,0:T(2,128)(2,1)}), bf16[64,2,128,64]{2,1,3,0:T(2,128)(2,1)}, u32[]{:S(2)}, u32[]{:S(2)}) async-start(bf16[64,2,128,64]{2,1,3,0:T(2,128)(2,1)} %copy.74), calls=%async_computation.5 | async-start | bytes 4194304 | tf_op jit(solution)/shard_map/all_to_all | solution.py:15
  252.2 1.0 reduce.1
  254.1 95.6 %all-to-all-done.5 = bf16[64,2,128,64]{2,1,3,0:T(2,128)(2,1)} async-done(((bf16[64,2,128,64]{2,1,3,0:T(2,128)(2,1)}), bf16[64,2,128,64]{2,1,3,0:T(2,128)(2,1)}, u32[]{:S(2)}, u32[]{:S(2)}) %all-to-all-start.5) | async-done | bytes 2097184 | tf_op jit(solution)/shard_map/all_to_all | solution.py:15
  349.7 3.9 %fusion.7 = bf16[8,128,64]{1,0,2:T(8,128)(2,1)S(1)} fusion(bf16[64,2,128,64]{2,1,3,0:T(2,128)(2,1)} %all-to-all-done.5, s32[64,2]{0,1:T(2,128)S(1)} %bitcast.106), kind=kOutput, calls=%fused_computation.15 | convolution fusion | flops 16843776 | bytes 2228736 | tf_op jit(solution)/shard_map/scb,scif->bif/dot_general | solution.py:97
  (53 shorter events, 11.1 us)
Async XLA Ops:
  7.2 101.9 %copy-start = (bf16[64,128,128]{2,1,0:T(8,128)(2,1)S(1)}, bf16[64,128,128]{2,1,0:T(8,128)(2,1)}, u32[]{:S(2)}) copy-start(bf16[64,128,128]{2,1,0:T(8,128)(2,1)} %param.9) | copy-start | bytes 6291460
  10.4 32.2 %all-to-all-start = ((s32[64,1,2]{2,1,0:T(1,128)}), s32[64,1,2]{2,1,0:T(1,128)S(1)}, u32[]{:S(2)}, u32[]{:S(2)}) async-start(s32[64,1,2]{2,1,0:T(1,128)} %copy.60), calls=%async_computation | async-start | bytes 65536 | tf_op jit(solution)/shard_map/all_to_all | solution.py:15
  48.4 6.5 %copy-start.2 = (s32[64,1]{0,1:T(1,128)S(1)}, s32[64,1]{0,1:T(1,128)}, u32[]{:S(2)}) copy-start(s32[64,1]{0,1:T(1,128)} %param.11) | copy-start | bytes 772
  48.4 58.7 %all-to-all-start.1 = ((bf16[64,2,128,32]{2,3,1,0:T(8,128)(2,1)}), bf16[64,2,128,32]{2,3,1,0:T(8,128)(2,1)}, u32[]{:S(2)}, u32[]{:S(2)}) async-start(bf16[64,2,128,32]{2,3,1,0:T(8,128)(2,1)} %get-tuple-element.24), calls=%async_computation.1 | async-start | bytes 2097152 | tf_op jit(solution)/shard_map/all_to_all | solution.py:15
  109.0 1.2 copy-start.1
  111.3 60.9 %all-to-all-start.2 = ((bf16[64,2,128,32]{2,3,1,0:T(8,128)(2,1)}), bf16[64,2,128,32]{2,3,1,0:T(8,128)(2,1)}, u32[]{:S(2)}, u32[]{:S(2)}) async-start(bf16[64,2,128,32]{2,3,1,0:T(8,128)(2,1)} %get-tuple-element.6), calls=%async_computation.2 | async-start | bytes 2097152 | tf_op jit(solution)/shard_map/all_to_all | solution.py:15
  118.8 107.8 %all-gather.3.cloned.1.call-start = ((), (), s32[]{:S(2)}) async-start(), calls=%async_computation.6 | async-start | bytes 1179648 | tf_op jit(solution)/shard_map/all_gather | solution.py:77
  175.3 14.8 %copy-start.3 = (s32[1024]{0:T(1024)S(1)}, s32[1024]{0:T(1024)}, u32[]{:S(2)}) copy-start(s32[1024]{0:T(1024)} %param.13) | copy-start | bytes 12292
  194.6 23.0 %all-to-all-start.3 = ((f32[64,1,512]{2,1,0:T(1,128)}), f32[64,1,512]{2,1,0:T(1,128)S(1)}, u32[]{:S(2)}, u32[]{:S(2)}) async-start(f32[64,1,512]{2,1,0:T(1,128)} %reshape.211), calls=%async_computation.3 | async-start | bytes 262144 | tf_op jit(solution)/shard_map/all_to_all | solution.py:15
  220.2 21.7 %all-to-all-start.4 = ((f32[64,1,512]{2,1,0:T(1,128)}), f32[64,1,512]{2,1,0:T(1,128)S(1)}, u32[]{:S(2)}, u32[]{:S(2)}) async-start(f32[64,1,512]{2,1,0:T(1,128)} %reshape.213), calls=%async_computation.4 | async-start | bytes 262144 | tf_op jit(solution)/shard_map/all_to_all | solution.py:24
  241.9 107.8 %all-to-all-start.5 = ((bf16[64,2,128,64]{2,1,3,0:T(2,128)(2,1)}), bf16[64,2,128,64]{2,1,3,0:T(2,128)(2,1)}, u32[]{:S(2)}, u32[]{:S(2)}) async-start(bf16[64,2,128,64]{2,1,3,0:T(2,128)(2,1)} %copy.74), calls=%async_computation.5 | async-start | bytes 4194304 | tf_op jit(solution)/shard_map/all_to_all | solution.py:15
Sparse Core Ops, SparseCore 0:
  191.3 22.9 all-gather.2
